TPU v7x, 512 devices: a whole 4x4x16 slice. The times are simulated.
512 devices in a mesh: ctx: 32 (over y, x, z_hi), head: 16 (over z_lo, core).
Axes of the slice: x: 4, y: 4, z: 16 (z_hi: 2, z_lo: 8; z = z_hi * 8 + z_lo), core: 2. Of those that a mesh axis runs over, the one named last changes fastest.
Arguments:
- tokens: bfloat16 [14336, 5376], P('ctx'), may hold values from -6 to 6
- w_query: bfloat16 [5376, 4096], P('ctx', 'head')
- key_weight: bfloat16 [5376, 2048], P('ctx', 'head')
- value_weight: bfloat16 [5376, 2048], P('ctx', 'head'), may hold values from -0.078125 to 0.078125
- query_gain: float32 [128], replicated, may hold values from 0.5 to 16
- key_gain: float32 [128], replicated, may hold values from 0.5 to 16
Outputs:
- attended: bfloat16 [14336, 4096], P('ctx', 'head')
All inputs are finite; a program needn't handle non-finite values.
Results may differ from a plain program's by a relative error of at most 0.025.
Values may be sent and summed in bfloat16 or wider, within the bound.
No kernel may reach another device: no remote copies, remote signals or barrier semaphores. Data moves between devices by JAX's collectives and lax.ppermute only.
A program may use at most 64 MiB of HBM per device.

v0:
```python
import jax
import jax.numpy as jnp
from jax import lax
from jax.sharding import PartitionSpec as P

WINDOW = 1024
query_scale = 168.0 ** (-0.5)


def from_behind(block, axis, distance):
    devices = range(lax.axis_size(axis))
    route = [(i - distance, i) for i in devices if i - distance in devices]
    return lax.ppermute(block, axis, route)


def normalize(values, gain):
    return values * lax.rsqrt(jnp.mean(values * values, axis=-1, keepdims=True) + 1e-06) * gain


def rotate(values, position):
    half = values.shape[-1] // 2
    expo = jnp.arange(half, dtype=jnp.float32) * (2.0 / values.shape[-1])
    freq = jnp.power(jnp.float32(10000.0), -expo)
    angle = position[:, None] * freq[None, :]
    cosine = jnp.cos(angle)[:, None, :]
    sine = jnp.sin(angle)[:, None, :]
    first = values[..., :half]
    second = values[..., half:]
    return jnp.concatenate(
        [first * cosine - second * sine, second * cosine + first * sine], axis=-1
    )


def fold_rows(tokens, piece):
    return jnp.dot(tokens, piece, preferred_element_type=jnp.float32)


def on_device(tokens, w_query, key_weight, value_weight, query_gain, key_gain):
    row_count = tokens.shape[0]
    head_size = query_gain.shape[0]
    kv_local = key_weight.shape[1] // head_size
    q_width = w_query.shape[1]

    def add_one(piece):
        return fold_rows(tokens, piece)

    query_sum = add_one(lax.all_gather(w_query, "ctx", axis=0, tiled=True))
    summed_keys = add_one(lax.all_gather(key_weight, "ctx", axis=0, tiled=True))
    summed_values = add_one(lax.all_gather(value_weight, "ctx", axis=0, tiled=True))
    offset = lax.axis_index("ctx") * row_count
    local_pos = offset + jnp.arange(row_count, dtype=jnp.int32)
    position = local_pos.astype(jnp.float32)
    queries = rotate(
        normalize(query_sum.reshape(row_count, 2 * kv_local, head_size), query_gain), position
    ).astype(jnp.bfloat16)
    keys = rotate(
        normalize(summed_keys.reshape(row_count, kv_local, head_size), key_gain), position
    ).astype(jnp.bfloat16)
    values = summed_values.reshape(row_count, kv_local, head_size).astype(jnp.bfloat16)
    reach = WINDOW - 1
    hop_count = (reach + row_count - 1) // row_count
    needed = [min(row_count, reach - distance * row_count) for distance in range(hop_count)]
    received = []
    carried = (keys, values)
    for distance in range(hop_count):
        arrived = from_behind((carried[0], carried[1]), "ctx", 1)
        received.append(arrived)
        if distance + 1 < hop_count:
            keep = needed[distance + 1]
            cut = needed[distance] - keep
            carried = (arrived[0][cut:], arrived[1][cut:])
    all_keys = jnp.concatenate([piece[0] for piece in reversed(received)] + [keys], axis=0)
    all_values = jnp.concatenate([piece[1] for piece in reversed(received)] + [values], axis=0)
    key_pos = offset - reach + jnp.arange(reach + row_count, dtype=jnp.int32)
    allowed = (
        (key_pos[None, :] <= local_pos[:, None])
        & (key_pos[None, :] > local_pos[:, None] - WINDOW)
        & (key_pos[None, :] >= 0)
    )
    grouped_heads = queries.reshape(row_count, kv_local, 2, head_size)
    scores = (
        jnp.einsum("bkgd,ckd->kgbc", grouped_heads, all_keys, preferred_element_type=jnp.float32)
        * query_scale
    )
    scores = jnp.where(allowed[None, None], scores, jnp.float32(-1e30))
    top = jnp.max(scores, axis=-1, keepdims=True)
    weights = jnp.exp(scores - top)
    probs = (weights / jnp.sum(weights, axis=-1, keepdims=True)).astype(jnp.bfloat16)
    mixed = jnp.einsum("kgbc,ckd->bkgd", probs, all_values, preferred_element_type=jnp.float32)
    return mixed.reshape(row_count, q_width).astype(jnp.bfloat16)


def solution(mesh):
    placed = (P("ctx", None), P("ctx", "head"), P("ctx", "head"), P("ctx", "head"), P(), P())
    return jax.shard_map(
        on_device, mesh=mesh, in_specs=placed, out_specs=P("ctx", "head"), check_vma=False
    )
```

profile of v0, /device:TPU:2, one launch (start us, length us, event | category | flops | bytes accessed | tf_op | source)
XLA Modules:
  0.0 406.5 jit_solution(15615109111452498067)
XLA Ops:
  6.5 0.0 copy-start.1
  6.5 0.0 all-gather.6.cloned.1.call-start
  6.5 0.7 all-gather.6.cloned.1.call-update
  7.3 0.0 all-gather.4.cloned.1.call-start
  7.3 0.7 all-gather.4.cloned.1.call-update
  8.0 0.0 all-gather.8.cloned.1.call-start
  8.1 0.7 all-gather.8.cloned.1.call-update
  8.8 123.6 %all-gather.6.cloned.1.call-done = bf16[5376,128]{1,0:T(8,128)(2,1)} async-done(((bf16[168,128]{1,0:T(8,128)(2,1)}), bf16[5376,128]{1,0:T(8,128)(2,1)}) %all-gather.6.cloned.1.call-update) | async-done | bytes 1376272 | tf_op jit(solution)/shard_map/all_gather | solution.py:48
  132.3 4.3 %multiply_reduce_fusion.1 = (f32[448]{0:T(512)S(1)}, f32[448,128]{1,0:T(8,128)S(1)}) fusion(bf16[448,5376]{1,0:T(8,128)(2,1)} %param.6, bf16[5376,128]{1,0:T(8,128)(2,1)} %all-gather.6.cloned.1.call-done), kind=kOutput, calls=%fused_computation.35 | convolution fusion | flops 616676928 | bytes 6424320 | tf_op jit(solution)/shard_map/dot_general | solution.py:35
  136.6 0.0 copy-done.1
  136.7 0.1 multiply_bitcast_fusion
  136.8 1.1 fusion.18
  137.9 0.1 pad_maximum_fusion
  138.0 1.9 collective-permute-start.3
  139.9 104.3 %all-gather.4.cloned.1.call-done = bf16[5376,128]{1,0:T(8,128)(2,1)} async-done(((bf16[168,128]{1,0:T(8,128)(2,1)}), bf16[5376,128]{1,0:T(8,128)(2,1)}) %all-gather.4.cloned.1.call-update) | async-done | bytes 1376272 | tf_op jit(solution)/shard_map/all_gather | solution.py:49
  244.2 4.2 %fusion.9 = bf16[448,1,128]{2,0,1:T(8,128)(2,1)S(1)} fusion(bf16[448,5376]{1,0:T(8,128)(2,1)} %param.6, bf16[5376,128]{1,0:T(8,128)(2,1)} %all-gather.4.cloned.1.call-done), kind=kOutput, calls=%fused_computation.10 | convolution fusion | flops 616620032 | bytes 6307840 | tf_op jit(solution)/shard_map/dot_general | solution.py:35
  248.4 1.9 collective-permute-start
  250.3 0.0 collective-permute-done.3
  250.4 13.2 %collective-permute-start.4 = (bf16[448,1,128]{2,0,1:T(8,128)(2,1)S(1)}, bf16[448,1,128]{2,0,1:T(8,128)(2,1)S(1)}, u32[]{:S(2)}, u32[]{:S(2)}) collective-permute-start(bf16[448,1,128]{2,0,1:T(8,128)(2,1)S(1)} %collective-permute-done.3), channel_id=1, source_target_pairs={{0,16},{16,32},{32,48},{48,64},{64,80},{80,96},{96,112},{112,128},... | collective-permute-start | bytes 344072 | tf_op jit(solution)/shard_map/ppermute | solution.py:13
  263.6 17.1 %collective-permute-done = bf16[448,1,128]{2,0,1:T(8,128)(2,1)S(1)} collective-permute-done((bf16[448,1,128]{2,0,1:T(8,128)(2,1)S(1)}, bf16[448,1,128]{2,0,1:T(8,128)(2,1)S(1)}, u32[]{:S(2)}, u32[]{:S(2)}) %collective-permute-start) | collective-permute-done | bytes 114720 | tf_op jit(solution)/shard_map/ppermute | solution.py:13
  280.7 1.9 collective-permute-start.1
  282.6 0.7 and_and_fusion
  283.4 5.9 %collective-permute-done.4 = bf16[448,1,128]{2,0,1:T(8,128)(2,1)S(1)} collective-permute-done((bf16[448,1,128]{2,0,1:T(8,128)(2,1)S(1)}, bf16[448,1,128]{2,0,1:T(8,128)(2,1)S(1)}, u32[]{:S(2)}, u32[]{:S(2)}) %collective-permute-start.4) | collective-permute-done | bytes 114720 | tf_op jit(solution)/shard_map/ppermute | solution.py:13
  289.3 7.0 %collective-permute-start.5 = (bf16[127,1,128]{2,0,1:T(8,128)(2,1)S(1)}, bf16[127,1,128]{2,0,1:T(8,128)(2,1)S(1)}, u32[]{:S(2)}, u32[]{:S(2)}) collective-permute-start(bf16[127,1,128]{2,0,1:T(8,128)(2,1)S(1)} %slice.27), channel_id=1, source_target_pairs={{0,16},{16,32},{32,48},{48,64},{64,80},{80,96},{96,112},{112,128},... | collective-permute-start | bytes 97544 | tf_op jit(solution)/shard_map/ppermute | solution.py:13
  296.2 2.6 collective-permute-done.1
  298.8 5.2 %collective-permute-start.2 = (bf16[127,1,128]{2,0,1:T(8,128)(2,1)S(1)}, bf16[127,1,128]{2,0,1:T(8,128)(2,1)S(1)}, u32[]{:S(2)}, u32[]{:S(2)}) collective-permute-start(bf16[127,1,128]{2,0,1:T(8,128)(2,1)S(1)} %slice.24), channel_id=1, source_target_pairs={{0,16},{16,32},{32,48},{48,64},{64,80},{80,96},{96,112},{112,128},... | collective-permute-start | bytes 97544 | tf_op jit(solution)/shard_map/ppermute | solution.py:13
  304.0 0.9 multiply_cosine_fusion
  304.9 0.5 collective-permute-done.5
  305.4 1.6 concatenate.26
  307.0 8.0 %collective-permute-done.2 = bf16[127,1,128]{2,0,1:T(8,128)(2,1)S(1)} collective-permute-done((bf16[127,1,128]{2,0,1:T(8,128)(2,1)S(1)}, bf16[127,1,128]{2,0,1:T(8,128)(2,1)S(1)}, u32[]{:S(2)}, u32[]{:S(2)}) %collective-permute-start.2) | collective-permute-done | bytes 32544 | tf_op jit(solution)/shard_map/ppermute | solution.py:13
  315.0 1.6 concatenate.24
  316.6 0.0 copy-start
  316.6 72.9 %all-gather.8.cloned.1.call-done = bf16[5376,256]{1,0:T(8,128)(2,1)} async-done(((bf16[168,256]{1,0:T(8,128)(2,1)}), bf16[5376,256]{1,0:T(8,128)(2,1)}) %all-gather.8.cloned.1.call-update) | async-done | bytes 2752528 | tf_op jit(solution)/shard_map/all_gather | solution.py:47
  389.5 4.6 %fusion.28 = f32[448,256]{1,0:T(8,128)S(1)} fusion(bf16[448,5376]{1,0:T(8,128)(2,1)} %param.6, bf16[5376,256]{1,0:T(8,128)(2,1)} %all-gather.8.cloned.1.call-done), kind=kOutput, calls=%fused_computation.47 | convolution fusion | flops 1233125376 | bytes 8028160 | tf_op jit(solution)/shard_map/dot_general | solution.py:35
  394.2 0.2 reshape.288
  394.4 0.5 multiply_reduce_fusion
  395.0 0.1 copy.13
  395.1 0.0 copy-done
  395.1 0.2 fusion.10
  395.3 0.2 subtract_convert_fusion
  395.6 1.5 fusion.27
  397.1 0.9 fusion
  398.0 1.0 fusion.6
  399.0 0.2 copy.15
  399.2 0.7 copy.20
  (9 shorter events, 0.1 us)
Async XLA Ops:
  6.5 130.1 %copy-start.1 = (f32[128]{0:T(128)S(1)}, f32[128]{0:T(128)}, u32[]{:S(2)}) copy-start(f32[128]{0:T(128)} %param.11) | copy-start | bytes 1540
  6.5 125.8 %all-gather.6.cloned.1.call-start = ((), (), s32[]{:S(2)}) async-start(), calls=%async_computation.1 | async-start | bytes 1419264 | tf_op jit(solution)/shard_map/all_gather | solution.py:48
  7.3 236.9 %all-gather.4.cloned.1.call-start = ((), (), s32[]{:S(2)}) async-start(), calls=%async_computation | async-start | bytes 1419264 | tf_op jit(solution)/shard_map/all_gather | solution.py:49
  8.0 381.5 %all-gather.8.cloned.1.call-start = ((), (), s32[]{:S(2)}) async-start(), calls=%async_computation.2 | async-start | bytes 2838528 | tf_op jit(solution)/shard_map/all_gather | solution.py:47
  138.0 112.4 %collective-permute-start.3 = (bf16[448,1,128]{2,0,1:T(8,128)(2,1)S(1)}, bf16[448,1,128]{2,0,1:T(8,128)(2,1)S(1)}, u32[]{:S(2)}, u32[]{:S(2)}) collective-permute-start(bf16[448,1,128]{2,0,1:T(8,128)(2,1)S(1)} %pad_maximum_fusion), channel_id=1, source_target_pairs={{0,16},{16,32},{32,48},{48,64},{64,80},{80,96},{96,112},{112,128},... | collective-permute-start | bytes 344072 | tf_op jit(solution)/shard_map/ppermute | solution.py:13
  248.4 32.3 %collective-permute-start = (bf16[448,1,128]{2,0,1:T(8,128)(2,1)S(1)}, bf16[448,1,128]{2,0,1:T(8,128)(2,1)S(1)}, u32[]{:S(2)}, u32[]{:S(2)}) collective-permute-start(bf16[448,1,128]{2,0,1:T(8,128)(2,1)S(1)} %fusion.9), channel_id=1, source_target_pairs={{0,16},{16,32},{32,48},{48,64},{64,80},{80,96},{96,112},{112,128},... | collective-permute-start | bytes 344072 | tf_op jit(solution)/shard_map/ppermute | solution.py:13
  250.4 38.9 %collective-permute-start.4 = (bf16[448,1,128]{2,0,1:T(8,128)(2,1)S(1)}, bf16[448,1,128]{2,0,1:T(8,128)(2,1)S(1)}, u32[]{:S(2)}, u32[]{:S(2)}) collective-permute-start(bf16[448,1,128]{2,0,1:T(8,128)(2,1)S(1)} %collective-permute-done.3), channel_id=1, source_target_pairs={{0,16},{16,32},{32,48},{48,64},{64,80},{80,96},{96,112},{112,128},... | collective-permute-start | bytes 344072 | tf_op jit(solution)/shard_map/ppermute | solution.py:13
  280.7 18.0 %collective-permute-start.1 = (bf16[448,1,128]{2,0,1:T(8,128)(2,1)S(1)}, bf16[448,1,128]{2,0,1:T(8,128)(2,1)S(1)}, u32[]{:S(2)}, u32[]{:S(2)}) collective-permute-start(bf16[448,1,128]{2,0,1:T(8,128)(2,1)S(1)} %collective-permute-done), channel_id=1, source_target_pairs={{0,16},{16,32},{32,48},{48,64},{64,80},{80,96},{96,112},{112,128},... | collective-permute-start | bytes 344072 | tf_op jit(solution)/shard_map/ppermute | solution.py:13
  289.3 16.1 %collective-permute-start.5 = (bf16[127,1,128]{2,0,1:T(8,128)(2,1)S(1)}, bf16[127,1,128]{2,0,1:T(8,128)(2,1)S(1)}, u32[]{:S(2)}, u32[]{:S(2)}) collective-permute-start(bf16[127,1,128]{2,0,1:T(8,128)(2,1)S(1)} %slice.27), channel_id=1, source_target_pairs={{0,16},{16,32},{32,48},{48,64},{64,80},{80,96},{96,112},{112,128},... | collective-permute-start | bytes 97544 | tf_op jit(solution)/shard_map/ppermute | solution.py:13
  298.8 16.2 %collective-permute-start.2 = (bf16[127,1,128]{2,0,1:T(8,128)(2,1)S(1)}, bf16[127,1,128]{2,0,1:T(8,128)(2,1)S(1)}, u32[]{:S(2)}, u32[]{:S(2)}) collective-permute-start(bf16[127,1,128]{2,0,1:T(8,128)(2,1)S(1)} %slice.24), channel_id=1, source_target_pairs={{0,16},{16,32},{32,48},{48,64},{64,80},{80,96},{96,112},{112,128},... | collective-permute-start | bytes 97544 | tf_op jit(solution)/shard_map/ppermute | solution.py:13
  316.6 78.5 %copy-start = (f32[128]{0:T(128)S(1)}, f32[128]{0:T(128)}, u32[]{:S(2)}) copy-start(f32[128]{0:T(128)} %param.10) | copy-start | bytes 1540
Sparse Core Ops, SparseCore 0:
  11.7 120.5 all-gather.5
  136.7 107.4 all-gather.3
  248.6 140.9 all-gather.7
where the time goes:
time: 407 us; the launch traced here: 406 us
  waiting for transfers between devices  337 us (83%)
  starting transfers between devices  31.2 us (8%)
  matrix products  15.6 us (4%)
  between operations  13.3 us (3%)
  other arithmetic  4.81 us (1%)
  local copies, waits for them, and re-layouts  4.53 us (1%)
    all_gather x1, waiting for transfers between devices, on_device(): summed_keys = add_one(lax.all_gather(key_weight, 'ctx', axis=0, tiled=True))  124 us
    all_gather x1, waiting for transfers between devices, on_device(): lax.all_gather(value_weight, 'ctx', axis=0, tiled=True)  104 us
    all_gather x1, waiting for transfers between devices, on_device(): query_sum = add_one(lax.all_gather(w_query, 'ctx', axis=0, tiled=True))  72.9 us
    ppermute x6, waiting for transfers between devices, from_behind(): return lax.ppermute(block, axis, route)  34.1 us
    ppermute x6, starting transfers between devices, from_behind(): return lax.ppermute(block, axis, route)  31.2 us
    dot_general x3, matrix products, fold_rows(): return jnp.dot(tokens, piece, preferred_element_type=jnp.float32)  13.1 us
  transfers between devices with their start and end apart: 9, of which 8 were waited for; matrix products, arithmetic and copies ran while one was open for 4% of the time, Pallas kernels for 0%

commit v1 on v0

--- a/solution.py
+++ b/solution.py
@@ -44,7 +44,11 @@
     def add_one(piece):
         return fold_rows(tokens, piece)
 
-    query_sum = add_one(lax.all_gather(w_query, "ctx", axis=0, tiled=True))
+    query_sum = add_one(
+        jnp.concatenate(
+            lax.all_to_all(jnp.stack([w_query] * lax.axis_size("ctx")), "ctx", 0, 0), axis=0
+        )
+    )
     summed_keys = add_one(lax.all_gather(key_weight, "ctx", axis=0, tiled=True))
     summed_values = add_one(lax.all_gather(value_weight, "ctx", axis=0, tiled=True))
     offset = lax.axis_index("ctx") * row_count

time: 407 us -> 432 us (1.061)
  the two profiles are of different devices: /device:TPU:2 before, /device:TPU:8 now
where the time goes in v1:
time: 432 us; the launch traced here: 431 us
  waiting for transfers between devices  324 us (75%)
  starting transfers between devices  52.8 us (12%)
  local copies, waits for them, and re-layouts  19.1 us (4%)
  matrix products  15.9 us (4%)
  between operations  13.7 us (3%)
  other arithmetic  5.09 us (1%)
    all_gather x1, waiting for transfers between devices, on_device(): summed_keys = add_one(lax.all_gather(key_weight, 'ctx', axis=0, tiled=True))  189 us
    all_gather x1, waiting for transfers between devices, on_device(): lax.all_gather(value_weight, 'ctx', axis=0, tiled=True)  104 us
    ppermute x6, starting transfers between devices, from_behind(): return lax.ppermute(block, axis, route)  31.9 us
    ppermute x6, waiting for transfers between devices, from_behind(): return lax.ppermute(block, axis, route)  29.9 us
    all_to_all x1, starting transfers between devices, on_device(): lax.all_to_all(jnp.stack([w_query] * lax.axis_size('ctx')), 'ctx', 0, 0)  20.8 us
    dot_general x3, matrix products, fold_rows(): return jnp.dot(tokens, piece, preferred_element_type=jnp.float32)  13.4 us
  transfers between devices with their start and end apart: 9, of which 5 were waited for; matrix products, arithmetic and copies ran while one was open for 6% of the time, Pallas kernels for 0%

profile of v1, /device:TPU:8, one launch (start us, length us, event | category | flops | bytes accessed | tf_op | source)
XLA Modules:
  0.0 431.0 jit_solution(4358996780785740960)
XLA Ops:
  6.5 2.6 stack.2
  9.2 20.8 %all-to-all-start = ((bf16[32,168,256]{2,1,0:T(8,128)(2,1)}), bf16[32,168,256]{2,1,0:T(8,128)(2,1)S(1)}, u32[]{:S(2)}, u32[]{:S(2)}) async-start(bf16[32,168,256]{2,1,0:T(8,128)(2,1)} %stack.2), calls=%async_computation | async-start | bytes 5505024 | tf_op jit(solution)/shard_map/all_to_all | solution.py:49
  30.0 0.0 copy-start.11
  30.0 0.0 all-gather.5.cloned.1.call-start
  30.0 0.7 all-gather.5.cloned.1.call-update
  30.7 0.0 all-gather.3.cloned.1.call-start
  30.7 0.7 all-gather.3.cloned.1.call-update
  31.5 0.0 copy-start.8
  31.5 0.0 copy-start.6
  31.5 188.9 %all-gather.5.cloned.1.call-done = bf16[5376,128]{1,0:T(8,128)(2,1)} async-done(((bf16[168,128]{1,0:T(8,128)(2,1)}), bf16[5376,128]{1,0:T(8,128)(2,1)}) %all-gather.5.cloned.1.call-update) | async-done | bytes 1376272 | tf_op jit(solution)/shard_map/all_gather | solution.py:52
  220.4 4.3 multiply_reduce_fusion.1
  224.7 0.0 copy-done.11
  224.7 0.1 multiply_bitcast_fusion
  224.9 1.1 fusion.19
  226.0 0.0 copy-done.8
  226.0 0.0 copy-done.6
  226.0 0.1 pad_maximum_fusion
  226.1 1.9 collective-permute-start.3
  228.0 104.3 %all-gather.3.cloned.1.call-done = bf16[5376,128]{1,0:T(8,128)(2,1)} async-done(((bf16[168,128]{1,0:T(8,128)(2,1)}), bf16[5376,128]{1,0:T(8,128)(2,1)}) %all-gather.3.cloned.1.call-update) | async-done | bytes 1376272 | tf_op jit(solution)/shard_map/all_gather | solution.py:53
  332.3 0.0 copy-start.7
  332.3 0.0 copy-start.9
  332.3 4.2 fusion.11
  336.5 0.0 copy-start.3
  336.5 1.9 collective-permute-start
  338.5 0.0 collective-permute-done.3
  338.5 0.0 copy-start.4
  338.5 12.7 %collective-permute-start.4 = (bf16[448,1,128]{2,0,1:T(8,128)(2,1)S(1)}, bf16[448,1,128]{2,0,1:T(8,128)(2,1)S(1)}, u32[]{:S(2)}, u32[]{:S(2)}) collective-permute-start(bf16[448,1,128]{2,0,1:T(8,128)(2,1)S(1)} %collective-permute-done.3), channel_id=1, source_target_pairs={{0,16},{16,32},{32,48},{48,64},{64,80},{80,96},{96,112},{112,128},... | collective-permute-start | bytes 344072 | tf_op jit(solution)/shard_map/ppermute | solution.py:13
  351.2 17.4 %collective-permute-done = bf16[448,1,128]{2,0,1:T(8,128)(2,1)S(1)} collective-permute-done((bf16[448,1,128]{2,0,1:T(8,128)(2,1)S(1)}, bf16[448,1,128]{2,0,1:T(8,128)(2,1)S(1)}, u32[]{:S(2)}, u32[]{:S(2)}) %collective-permute-start) | collective-permute-done | bytes 114720 | tf_op jit(solution)/shard_map/ppermute | solution.py:13
  368.6 0.0 copy-start.5
  368.6 1.9 collective-permute-start.1
  370.5 1.5 and_and_fusion
  372.1 0.0 collective-permute-done.4
  372.1 11.6 %collective-permute-start.5 = (bf16[127,1,128]{2,0,1:T(8,128)(2,1)S(1)}, bf16[127,1,128]{2,0,1:T(8,128)(2,1)}, u32[]{:S(2)}, u32[]{:S(2)}) collective-permute-start(bf16[127,1,128]{2,0,1:T(8,128)(2,1)S(1)} %slice.27), channel_id=1, source_target_pairs={{0,16},{16,32},{32,48},{48,64},{64,80},{80,96},{96,112},{112,128},... | collective-permute-start | bytes 97544 | tf_op jit(solution)/shard_map/ppermute | solution.py:13
  383.7 3.3 collective-permute-done.1
  387.0 0.6 slice.24
  387.6 0.0 copy-done.3
  387.7 0.0 copy-done.4
  387.7 0.0 copy-done.5
  387.7 1.9 collective-permute-start.2
  389.6 0.0 copy-done.7
  389.6 0.0 copy-done.9
  389.6 0.9 multiply_cosine_fusion
  390.5 0.0 collective-permute-done.5
  390.5 5.9 %concatenate.26 = bf16[1471,1,128]{2,0,1:T(8,128)(2,1)} concatenate(bf16[127,1,128]{2,0,1:T(8,128)(2,1)} %collective-permute-done.5, bf16[448,1,128]{2,0,1:T(8,128)(2,1)S(1)} %collective-permute-done.4, bf16[448,1,128]{2,0,1:T(8,128)(2,1)} %copy-done.4, bf16[448,1,128]{2,0,1:T(8,128)(2,1)S(1)} %pad_maximum_fusion), dimensions={0} | concatenate | bytes 753152 | tf_op jit(solution)/shard_map/concatenate | solution.py:76
  396.4 9.1 %collective-permute-done.2 = bf16[127,1,128]{2,0,1:T(8,128)(2,1)} collective-permute-done((bf16[127,1,128]{2,0,1:T(8,128)(2,1)}, bf16[127,1,128]{2,0,1:T(8,128)(2,1)}, u32[]{:S(2)}, u32[]{:S(2)}) %collective-permute-start.2) | collective-permute-done | bytes 32544 | tf_op jit(solution)/shard_map/ppermute | solution.py:13
  405.5 6.0 %concatenate.24 = bf16[1471,1,128]{2,0,1:T(8,128)(2,1)} concatenate(bf16[127,1,128]{2,0,1:T(8,128)(2,1)} %collective-permute-done.2, bf16[448,1,128]{2,0,1:T(8,128)(2,1)S(1)} %collective-permute-done.1, bf16[448,1,128]{2,0,1:T(8,128)(2,1)} %copy-done.5, bf16[448,1,128]{2,0,1:T(8,128)(2,1)} %copy-done.3), dimensions={0} | concatenate | bytes 753152 | tf_op jit(solution)/shard_map/concatenate | solution.py:77
  411.5 0.0 all-to-all-done
  411.5 3.0 copy.8
  414.4 0.0 copy-start.10
  414.4 0.0 copy-start
  414.4 0.0 copy-start.1
  414.4 4.9 %multiply_reduce_fusion = (f32[448,2]{0,1:T(2,128)S(1)}, f32[448,2,128]{2,0,1:T(8,128)S(1)}) fusion(bf16[2,128,5376]{2,1,0:T(8,128)(2,1)} %bitcast.50, bf16[448,5376]{1,0:T(8,128)(2,1)} %param.6), kind=kOutput, calls=%fused_computation.16 | convolution fusion | flops 1233353856 | bytes 8031744 | tf_op jit(solution)/shard_map/dot_general | solution.py:35
  419.4 0.0 copy-done.10
  419.4 0.2 multiply_multiply_fusion
  419.6 0.2 subtract_convert_fusion
  419.8 0.0 copy-done
  419.8 0.0 copy-done.1
  419.8 0.0 copy-start.2
  419.8 1.5 fusion.28
  421.3 0.9 fusion
  422.2 0.0 copy-done.2
  422.3 1.0 fusion.8
  423.2 0.2 copy.9
  423.5 0.7 copy.12
  (8 shorter events, 0.1 us)
Async XLA Ops:
  9.2 402.3 %all-to-all-start = ((bf16[32,168,256]{2,1,0:T(8,128)(2,1)}), bf16[32,168,256]{2,1,0:T(8,128)(2,1)S(1)}, u32[]{:S(2)}, u32[]{:S(2)}) async-start(bf16[32,168,256]{2,1,0:T(8,128)(2,1)} %stack.2), calls=%async_computation | async-start | bytes 5505024 | tf_op jit(solution)/shard_map/all_to_all | solution.py:49
  30.0 194.8 %copy-start.11 = (f32[128]{0:T(128)S(1)}, f32[128]{0:T(128)}, u32[]{:S(2)}) copy-start(f32[128]{0:T(128)} %param.11) | copy-start | bytes 1540
  30.0 190.5 %all-gather.5.cloned.1.call-start = ((), (), s32[]{:S(2)}) async-start(), calls=%async_computation.2 | async-start | bytes 1419264 | tf_op jit(solution)/shard_map/all_gather | solution.py:52
  30.7 301.6 %all-gather.3.cloned.1.call-start = ((), (), s32[]{:S(2)}) async-start(), calls=%async_computation.1 | async-start | bytes 1419264 | tf_op jit(solution)/shard_map/all_gather | solution.py:53
  31.5 194.5 %copy-start.8 = (f32[64]{0:T(128)}, f32[64]{0:T(128)S(1)}, u32[]{:S(2)}) copy-start(f32[64]{0:T(128)S(1)} %negate_power_fusion) | copy-start | bytes 772
  31.5 194.5 %copy-start.6 = (f32[448]{0:T(512)}, f32[448]{0:T(512)S(1)}, u32[]{:S(2)}) copy-start(f32[448]{0:T(512)S(1)} %fusion.25) | copy-start | bytes 5380
  226.1 112.4 %collective-permute-start.3 = (bf16[448,1,128]{2,0,1:T(8,128)(2,1)S(1)}, bf16[448,1,128]{2,0,1:T(8,128)(2,1)S(1)}, u32[]{:S(2)}, u32[]{:S(2)}) collective-permute-start(bf16[448,1,128]{2,0,1:T(8,128)(2,1)S(1)} %pad_maximum_fusion), channel_id=1, source_target_pairs={{0,16},{16,32},{32,48},{48,64},{64,80},{80,96},{96,112},{112,128},... | collective-permute-start | bytes 344072 | tf_op jit(solution)/shard_map/ppermute | solution.py:13
  332.3 57.3 %copy-start.7 = (f32[448]{0:T(512)S(1)}, f32[448]{0:T(512)}, u32[]{:S(2)}) copy-start(f32[448]{0:T(512)} %copy-done.6) | copy-start | bytes 5380
  332.3 57.3 %copy-start.9 = (f32[64]{0:T(128)S(1)}, f32[64]{0:T(128)}, u32[]{:S(2)}) copy-start(f32[64]{0:T(128)} %copy-done.8) | copy-start | bytes 772
  336.5 51.1 %copy-start.3 = (bf16[448,1,128]{2,0,1:T(8,128)(2,1)}, bf16[448,1,128]{2,0,1:T(8,128)(2,1)S(1)}, u32[]{:S(2)}) copy-start(bf16[448,1,128]{2,0,1:T(8,128)(2,1)S(1)} %fusion.11) | copy-start | bytes 344068
  336.5 32.1 %collective-permute-start = (bf16[448,1,128]{2,0,1:T(8,128)(2,1)S(1)}, bf16[448,1,128]{2,0,1:T(8,128)(2,1)S(1)}, u32[]{:S(2)}, u32[]{:S(2)}) collective-permute-start(bf16[448,1,128]{2,0,1:T(8,128)(2,1)S(1)} %fusion.11), channel_id=1, source_target_pairs={{0,16},{16,32},{32,48},{48,64},{64,80},{80,96},{96,112},{112,128},... | collective-permute-start | bytes 344072 | tf_op jit(solution)/shard_map/ppermute | solution.py:13
  338.5 49.2 %copy-start.4 = (bf16[448,1,128]{2,0,1:T(8,128)(2,1)}, bf16[448,1,128]{2,0,1:T(8,128)(2,1)S(1)}, u32[]{:S(2)}) copy-start(bf16[448,1,128]{2,0,1:T(8,128)(2,1)S(1)} %collective-permute-done.3) | copy-start | bytes 344068
  338.5 33.6 %collective-permute-start.4 = (bf16[448,1,128]{2,0,1:T(8,128)(2,1)S(1)}, bf16[448,1,128]{2,0,1:T(8,128)(2,1)S(1)}, u32[]{:S(2)}, u32[]{:S(2)}) collective-permute-start(bf16[448,1,128]{2,0,1:T(8,128)(2,1)S(1)} %collective-permute-done.3), channel_id=1, source_target_pairs={{0,16},{16,32},{32,48},{48,64},{64,80},{80,96},{96,112},{112,128},... | collective-permute-start | bytes 344072 | tf_op jit(solution)/shard_map/ppermute | solution.py:13
  368.6 19.1 %copy-start.5 = (bf16[448,1,128]{2,0,1:T(8,128)(2,1)}, bf16[448,1,128]{2,0,1:T(8,128)(2,1)S(1)}, u32[]{:S(2)}) copy-start(bf16[448,1,128]{2,0,1:T(8,128)(2,1)S(1)} %collective-permute-done) | copy-start | bytes 344068
  368.6 18.4 %collective-permute-start.1 = (bf16[448,1,128]{2,0,1:T(8,128)(2,1)S(1)}, bf16[448,1,128]{2,0,1:T(8,128)(2,1)S(1)}, u32[]{:S(2)}, u32[]{:S(2)}) collective-permute-start(bf16[448,1,128]{2,0,1:T(8,128)(2,1)S(1)} %collective-permute-done), channel_id=1, source_target_pairs={{0,16},{16,32},{32,48},{48,64},{64,80},{80,96},{96,112},{112,128},... | collective-permute-start | bytes 344072 | tf_op jit(solution)/shard_map/ppermute | solution.py:13
  372.1 18.4 %collective-permute-start.5 = (bf16[127,1,128]{2,0,1:T(8,128)(2,1)S(1)}, bf16[127,1,128]{2,0,1:T(8,128)(2,1)}, u32[]{:S(2)}, u32[]{:S(2)}) collective-permute-start(bf16[127,1,128]{2,0,1:T(8,128)(2,1)S(1)} %slice.27), channel_id=1, source_target_pairs={{0,16},{16,32},{32,48},{48,64},{64,80},{80,96},{96,112},{112,128},... | collective-permute-start | bytes 97544 | tf_op jit(solution)/shard_map/ppermute | solution.py:13
  387.7 17.8 %collective-permute-start.2 = (bf16[127,1,128]{2,0,1:T(8,128)(2,1)}, bf16[127,1,128]{2,0,1:T(8,128)(2,1)}, u32[]{:S(2)}, u32[]{:S(2)}) collective-permute-start(bf16[127,1,128]{2,0,1:T(8,128)(2,1)} %slice.24), channel_id=1, source_target_pairs={{0,16},{16,32},{32,48},{48,64},{64,80},{80,96},{96,112},{112,128},... | collective-permute-start | bytes 97544 | tf_op jit(solution)/shard_map/ppermute | solution.py:13
  414.4 5.0 %copy-start.10 = (f32[128]{0:T(128)S(1)}, f32[128]{0:T(128)}, u32[]{:S(2)}) copy-start(f32[128]{0:T(128)} %param.10) | copy-start | bytes 1540
  414.4 5.4 %copy-start = (pred[448,1471]{1,0:T(8,128)(4,1)S(1)}, pred[448,1471]{1,0:T(8,128)(4,1)}, u32[]{:S(2)}) copy-start(pred[448,1471]{1,0:T(8,128)(4,1)} %and_and_fusion) | copy-start | bytes 1977028
  414.4 5.4 %copy-start.1 = (bf16[1471,1,128]{2,0,1:T(8,128)(2,1)S(1)}, bf16[1471,1,128]{2,0,1:T(8,128)(2,1)}, u32[]{:S(2)}) copy-start(bf16[1471,1,128]{2,0,1:T(8,128)(2,1)} %concatenate.26) | copy-start | bytes 1129732
  419.8 2.4 copy-start.2
Sparse Core Ops, SparseCore 0:
  35.2 185.1 all-gather.4
  224.8 107.4 all-gather.2
